TPU v7x, 32 devices: a whole 2x2x4 slice. The times are simulated.
32 devices in a mesh: row: 8 (over y, x, core), col: 4 (over z).
Axes of the slice: x: 2, y: 2, z: 4, core: 2. Of those that a mesh axis runs over, the one named last changes fastest.
Arguments:
- sequence: bfloat16 [32768, 1536], P(('row', 'col')), may hold values from -6 to 6
- filter_weight: bfloat16 [3, 1536, 1536], replicated, may hold values from -0.09375 to 0.09375
- pair_proj: bfloat16 [1536, 256], replicated, may hold values from -0.15625 to 0.15625
- pair_out: bfloat16 [128, 128], replicated, may hold values from -0.5 to 0.5
- donor_w: bfloat16 [1536, 128], replicated, may hold values from -0.15625 to 0.15625
- donor_pos: int32 [8192], P(('row', 'col')), may hold values from 0 to 1023
- acceptor_bin: int32 [8192], P(('row', 'col')), may hold values from 0 to 255, as said below
Outputs:
- pair: bfloat16 [256, 256, 128], P('row', 'col')
- junctions: bfloat16 [8192, 128], P(('row', 'col'))
Inputs may be any that keep to these rules, and one draw needn't show every extreme that they name: Among the 256 junctions of one device at most 64 have acceptor_bin in any one block of 64 pair columns; on every device some block holds exactly 64.
All inputs are finite; a program needn't handle non-finite values.
Results may differ from a plain program's by a relative error of at most 0.013.
Values may be sent and summed in bfloat16 or wider, within the bound.
A program may use at most 128 MiB of HBM per device.

v0:
```python
import jax
import jax.numpy as jnp
from jax import lax
from jax.sharding import PartitionSpec as P

D = 1536
PCH = 128
DILATION_STEP = 32
POOL = 128
CAP = 64


def with_halo(cells, sides, width):
    for axis, dim in sides:
        count = lax.axis_size(axis)
        ends = count - 1
        head = lax.slice_in_dim(cells, 0, width, axis=dim)
        tail = lax.slice_in_dim(cells, cells.shape[dim] - width, cells.shape[dim], axis=dim)
        cells = jnp.concatenate(
            [
                lax.ppermute(tail, axis, [(i, (i + 1) % count) for i in range(ends)]),
                cells,
                lax.ppermute(head, axis, [((i + 1) % count, i) for i in range(ends)]),
            ],
            axis=dim,
        )
    return cells


def local(sequence, filter_weight, pair_proj, pair_out, donor_w, donor_pos, acceptor_bin):
    sequence_rows = sequence.shape[0]
    padded_sequence = with_halo(sequence, ((("row", "col"), 0),), DILATION_STEP)
    filtered_rows = jnp.dot(
        padded_sequence[0:sequence_rows], filter_weight[0], preferred_element_type=jnp.float32
    )
    filtered_rows = filtered_rows + jnp.dot(
        padded_sequence[DILATION_STEP : DILATION_STEP + sequence_rows],
        filter_weight[1],
        preferred_element_type=jnp.float32,
    )
    filtered_rows = filtered_rows + jnp.dot(
        padded_sequence[2 * DILATION_STEP : 2 * DILATION_STEP + sequence_rows],
        filter_weight[2],
        preferred_element_type=jnp.float32,
    )
    hidden = (sequence.astype(jnp.float32) + jax.nn.silu(filtered_rows)).astype(jnp.bfloat16)
    pooled = jnp.mean(hidden.reshape(sequence_rows // POOL, POOL, D), axis=1, dtype=jnp.float32)
    normed = (pooled * lax.rsqrt(jnp.mean(pooled * pooled, axis=-1, keepdims=True) + 1e-06)).astype(
        jnp.bfloat16
    )
    bins_local = sequence_rows // POOL
    row_count = lax.axis_size("row")
    col_count = lax.axis_size("col")
    row_index = lax.axis_index("row")
    col_index = lax.axis_index("col")
    tile_rows = bins_local * col_count
    tile_cols = bins_local * row_count
    gathered = lax.all_gather(normed, ("row", "col"), axis=0, tiled=True)
    row_feat = lax.dynamic_slice_in_dim(gathered, row_index * tile_rows, tile_rows, 0)
    col_feat = lax.dynamic_slice_in_dim(gathered, col_index * tile_cols, tile_cols, 0)
    row_side = jnp.dot(row_feat, pair_proj[:, :PCH], preferred_element_type=jnp.float32).astype(
        jnp.bfloat16
    )
    col_side = jnp.dot(col_feat, pair_proj[:, PCH:], preferred_element_type=jnp.float32).astype(
        jnp.bfloat16
    )
    pair_hidden = jax.nn.relu(
        row_side.astype(jnp.float32)[:, None, :] + col_side.astype(jnp.float32)[None, :, :]
    ).astype(jnp.bfloat16)
    pair_flat = jnp.dot(
        pair_hidden.reshape(tile_rows * tile_cols, PCH),
        pair_out,
        preferred_element_type=jnp.float32,
    ).astype(jnp.bfloat16)
    pair = pair_flat.reshape(tile_rows, tile_cols, PCH)
    sender = row_index * col_count + col_index
    col_group = acceptor_bin // tile_cols
    onehot = (col_group[:, None] == jnp.arange(col_count, dtype=jnp.int32)[None, :]).astype(
        jnp.int32
    )
    slot_rank = jnp.sum((jnp.cumsum(onehot, axis=0) - onehot) * onehot, axis=1)
    slot_index = col_group * CAP + slot_rank
    pair_row = (sender * sequence_rows + donor_pos) // POOL - row_index * tile_rows
    pair_col = acceptor_bin - col_group * tile_cols
    slot_total_count = col_count * CAP
    row_buffer = jnp.full((slot_total_count,), -1, jnp.int32).at[slot_index].set(pair_row)
    col_buffer = jnp.full((slot_total_count,), -1, jnp.int32).at[slot_index].set(pair_col)
    donor_rows = jnp.take(hidden, donor_pos, axis=0)
    send_rows = jnp.zeros((slot_total_count, D), jnp.bfloat16).at[slot_index].set(donor_rows)
    got_rows, got_pair_row, got_pair_col = (
        lax.all_to_all(send_rows, "col", split_axis=0, concat_axis=0, tiled=True),
        lax.all_to_all(row_buffer, "col", split_axis=0, concat_axis=0, tiled=True),
        lax.all_to_all(col_buffer, "col", split_axis=0, concat_axis=0, tiled=True),
    )
    donor_emb = jnp.dot(got_rows, donor_w, preferred_element_type=jnp.float32).astype(jnp.bfloat16)
    filled = got_pair_row >= 0
    flat_index = jnp.where(filled, got_pair_row * tile_cols + got_pair_col, 0)
    looked = jnp.take(pair_flat, flat_index, axis=0)
    junction_value = jax.nn.relu(donor_emb.astype(jnp.float32) + looked.astype(jnp.float32))
    junctions = jnp.where(filled[:, None], junction_value, 0.0).astype(jnp.bfloat16)
    return (pair, junctions)


def solution(mesh):
    placed = (P(("row", "col"), None), P(), P(), P(), P(), P(("row", "col")), P(("row", "col")))
    return jax.shard_map(
        local,
        mesh=mesh,
        in_specs=placed,
        out_specs=(P("row", "col", None), P(("row", "col"), None)),
        check_vma=False,
    )
```

profile of v0, /device:TPU:0, one launch (start us, length us, event | category | flops | bytes accessed | tf_op | source)
XLA Modules:
  0.0 161.7 jit_solution(15729254648578059642)
XLA Ops:
  0.6 1.0 fusion.44
  1.7 1.3 collective-permute-start.1
  3.0 5.6 %collective-permute-start = (bf16[32,1536]{1,0:T(8,128)(2,1)S(1)}, bf16[32,1536]{1,0:T(8,128)(2,1)S(1)}, u32[]{:S(2)}, u32[]{:S(2)}) collective-permute-start(bf16[32,1536]{1,0:T(8,128)(2,1)S(1)} %get-tuple-element.7), channel_id=1, source_target_pairs={{0,1},{1,2},{2,3},{3,4},{4,5},{5,6},{6,7},{7,8},{8,9},{9,10},{10,1... | collective-permute-start | bytes 294920 | tf_op jit(solution)/shard_map/ppermute | solution.py:21
  8.5 0.7 multiply_subtract_fusion
  9.2 1.2 reduce-window.6
  10.5 0.1 copy.17
  10.7 0.1 copy.18
  10.9 1.4 scatter_custom_fusion.2
  12.3 0.7 all_to_all.25
  12.9 6.8 %all-to-all-start.2 = ((s32[4,64,1]{1,2,0:T(1,128)}), s32[4,64,1]{1,2,0:T(1,128)S(1)}, u32[]{:S(2)}, u32[]{:S(2)}) async-start(s32[4,64,1]{1,2,0:T(1,128)} %bitcast.12), calls=%async_computation.2 | async-start | bytes 4096 | tf_op jit(solution)/shard_map/all_to_all | solution.py:93
  19.8 9.7 %fusion.2 = f32[1024,1536]{1,0:T(8,128)} fusion(bf16[1024,1536]{1,0:T(8,128)(2,1)} %param.7, bf16[3,1536,1536]{2,1,0:T(8,128)(2,1)} %param.8), kind=kOutput, calls=%fused_computation.9 | convolution fusion | flops 4831838208 | bytes 14155776 | tf_op jit(solution)/shard_map/dot_general | solution.py:36
  29.5 0.5 compare_and_fusion.1
  30.1 1.4 scatter_custom_fusion
  31.5 0.7 all_to_all.20
  32.1 5.1 %all-to-all-start = ((s32[4,64,1]{1,2,0:T(1,128)}), s32[4,64,1]{1,2,0:T(1,128)S(1)}, u32[]{:S(2)}, u32[]{:S(2)}) async-start(s32[4,64,1]{1,2,0:T(1,128)} %bitcast.9), calls=%async_computation | async-start | bytes 4096 | tf_op jit(solution)/shard_map/all_to_all | solution.py:92
  37.2 5.5 %all-to-all-done = s32[4,64,1]{1,2,0:T(1,128)S(1)} async-done(((s32[4,64,1]{1,2,0:T(1,128)}), s32[4,64,1]{1,2,0:T(1,128)S(1)}, u32[]{:S(2)}, u32[]{:S(2)}) %all-to-all-start) | async-done | bytes 1056 | tf_op jit(solution)/shard_map/all_to_all | solution.py:92
  42.7 0.1 select_n.78
  42.8 0.1 ge.36
  43.0 0.6 compare_and_fusion
  43.6 8.0 %fusion.4 = f32[1024,1536]{1,0:T(8,128)S(1)} fusion(bf16[3,1536,1536]{2,1,0:T(8,128)(2,1)} %param.8, bf16[1024,1536]{1,0:T(8,128)(2,1)} %param.7, bf16[32,1536]{1,0:T(8,128)(2,1)S(1)} %collective-permute-done), kind=kOutput, calls=%fused_computation.11 | convolution fusion | flops 4838129664 | bytes 14254080 | tf_op jit(solution)/shard_map/dot_general | solution.py:33
  51.6 10.2 %convert_reduce_fusion = (f32[8,1536]{1,0:T(8,128)S(1)}, bf16[1024,1536]{1,0:T(8,128)(2,1)S(1)}) fusion(bf16[3,1536,1536]{2,1,0:T(8,128)(2,1)} %param.8, bf16[32,1536]{1,0:T(8,128)(2,1)} %collective-permute-done.1, bf16[1024,1536]{1,0:T(8,128)(2,1)S(1)} %copy-done.2, f32[1024,1536]{1,0:T(8,128)S(1)} %fusion.4, f32[1024,1536]{1,0:T(8,128)} %fusion.2), kind=kOutput, calls=%fused_computation.5 | convolution fusion | flops 4855418880 | bytes 26886144 | tf_op jit(solution)/shard_map/dot_general | solution.py:41
  61.8 0.1 multiply_reduce_fusion
  61.9 0.7 multiply_convert_fusion
  62.6 5.4 %scatter_custom_fusion.1 = bf16[256,1536]{1,0:T(8,128)(2,1)} fusion(s32[256]{0:T(256)S(1)} %compare_select_fusion.4, pred[256]{0:T(512)(128)(4,1)} %compare_and_fusion.1, bf16[]{:T(256)} %constant.98.clone.1, bf16[]{:T(256)} %constant.96.clone.1, bf16[1024,1536]{1,0:T(8,128)(2,1)S(1)} %get-tuple-element.11, s32[1024]{0:T(1024)S(1)} %pad_clamp_fusion.1), kind=kCustom, calls=%fused_computation.32 | custom fusion | flops 393216 | bytes 3936516 | tf_op jit(solution)/shard_map/scatter | solution.py:89
  68.0 3.5 %all-to-all-start.1 = ((bf16[4,64,1536]{2,1,0:T(8,128)(2,1)}), bf16[4,64,1536]{2,1,0:T(8,128)(2,1)S(1)}, u32[]{:S(2)}, u32[]{:S(2)}) async-start(bf16[4,64,1536]{2,1,0:T(8,128)(2,1)} %bitcast.48), calls=%async_computation.1 | async-start | bytes 1572864 | tf_op jit(solution)/shard_map/all_to_all | solution.py:91
  71.5 84.1 %all_gather.3 = bf16[256,1536]{1,0:T(8,128)(2,1)S(1)} all-gather(bf16[8,1536]{1,0:T(8,128)(2,1)} %multiply_convert_fusion), channel_id=1, replica_groups=mesh['row'=8,'col'=4] {'row','col'}, dimensions={0}, use_global_device_ids=true | all-gather | bytes 811008 | tf_op jit(solution)/shard_map/all_gather | solution.py:58
  155.6 1.2 fusion.19
  156.8 1.2 fusion.18
  158.0 0.1 maximum_convert_fusion
  158.2 1.0 convolution_convert_fusion
  159.2 0.9 gather_fusion
  160.1 1.7 %fusion.17 = bf16[256,128]{1,0:T(8,128)(2,1)} fusion(bf16[256,1536]{1,0:T(8,128)(2,1)S(1)} %bitcast.51, bf16[1536,128]{1,0:T(8,128)(2,1)S(1)} %copy-done, bf16[256,128]{1,0:T(8,128)(2,1)S(1)} %gather_fusion, pred[256]{0:T(512)(128)(4,1)} %compare_and_fusion, pred[256]{0:T(512)(128)(4,1)S(1)} %ge.36), kind=kOutput, calls=%fused_computation.26 | convolution fusion | flops 100925440 | bytes 1311232 | tf_op jit(solution)/shard_map/dot_general | solution.py:95
  (27 shorter events, 0.4 us)
Async XLA Ops:
  0.6 159.4 %copy-start = (bf16[1536,128]{1,0:T(8,128)(2,1)S(1)}, bf16[1536,128]{1,0:T(8,128)(2,1)}, u32[]{:S(2)}) copy-start(bf16[1536,128]{1,0:T(8,128)(2,1)} %param.11) | copy-start | bytes 1179652
  1.7 49.9 %collective-permute-start.1 = (bf16[32,1536]{1,0:T(8,128)(2,1)S(1)}, bf16[32,1536]{1,0:T(8,128)(2,1)}, u32[]{:S(2)}, u32[]{:S(2)}) collective-permute-start(bf16[32,1536]{1,0:T(8,128)(2,1)S(1)} %get-tuple-element.6), channel_id=1, source_target_pairs={{1,0},{2,1},{3,2},{4,3},{5,4},{6,5},{7,6},{8,7},{9,8},{10,9},{11,1... | collective-permute-start | bytes 294920 | tf_op jit(solution)/shard_map/ppermute | solution.py:23
  3.0 40.6 %collective-permute-start = (bf16[32,1536]{1,0:T(8,128)(2,1)S(1)}, bf16[32,1536]{1,0:T(8,128)(2,1)S(1)}, u32[]{:S(2)}, u32[]{:S(2)}) collective-permute-start(bf16[32,1536]{1,0:T(8,128)(2,1)S(1)} %get-tuple-element.7), channel_id=1, source_target_pairs={{0,1},{1,2},{2,3},{3,4},{4,5},{5,6},{6,7},{7,8},{8,9},{9,10},{10,1... | collective-permute-start | bytes 294920 | tf_op jit(solution)/shard_map/ppermute | solution.py:21
  12.9 19.2 %all-to-all-start.2 = ((s32[4,64,1]{1,2,0:T(1,128)}), s32[4,64,1]{1,2,0:T(1,128)S(1)}, u32[]{:S(2)}, u32[]{:S(2)}) async-start(s32[4,64,1]{1,2,0:T(1,128)} %bitcast.12), calls=%async_computation.2 | async-start | bytes 4096 | tf_op jit(solution)/shard_map/all_to_all | solution.py:93
  19.8 9.7 %copy-start.3 = (s32[256]{0:T(256)S(1)}, s32[256]{0:T(256)}, u32[]{:S(2)}) copy-start(s32[256]{0:T(256)} %param.12) | copy-start | bytes 3076
  32.1 10.6 %all-to-all-start = ((s32[4,64,1]{1,2,0:T(1,128)}), s32[4,64,1]{1,2,0:T(1,128)S(1)}, u32[]{:S(2)}, u32[]{:S(2)}) async-start(s32[4,64,1]{1,2,0:T(1,128)} %bitcast.9), calls=%async_computation | async-start | bytes 4096 | tf_op jit(solution)/shard_map/all_to_all | solution.py:92
  43.6 8.0 %copy-start.2 = (bf16[1024,1536]{1,0:T(8,128)(2,1)S(1)}, bf16[1024,1536]{1,0:T(8,128)(2,1)}, u32[]{:S(2)}) copy-start(bf16[1024,1536]{1,0:T(8,128)(2,1)} %param.7) | copy-start | bytes 9437188
  68.0 92.1 %all-to-all-start.1 = ((bf16[4,64,1536]{2,1,0:T(8,128)(2,1)}), bf16[4,64,1536]{2,1,0:T(8,128)(2,1)S(1)}, u32[]{:S(2)}, u32[]{:S(2)}) async-start(bf16[4,64,1536]{2,1,0:T(8,128)(2,1)} %bitcast.48), calls=%async_computation.1 | async-start | bytes 1572864 | tf_op jit(solution)/shard_map/all_to_all | solution.py:91
  159.2 2.5 %copy-start.1 = (bf16[2048,128]{1,0:T(8,128)(2,1)}, bf16[2048,128]{1,0:T(8,128)(2,1)S(1)}, u32[]{:S(2)}) copy-start(bf16[2048,128]{1,0:T(8,128)(2,1)S(1)} %convolution_convert_fusion) | copy-start | bytes 1572868
where the time goes:
time: 162 us
  blocking collectives  84.1 us (52%)
  matrix products  33 us (20%)
  starting transfers between devices  22.3 us (14%)
  other arithmetic  9.59 us (6%)
  local copies, waits for them, and re-layouts  6.52 us (4%)
  waiting for transfers between devices  5.47 us (3%)
    all_gather x1, blocking collectives, local(): gathered = lax.all_gather(normed, ('row', 'col'), axis=0, tiled=True)  84.1 us
    dot_general x1, matrix products, local(): jnp.dot(padded_sequence[2 * DILATION_STEP:2 * DILATION_STEP + sequence_ro...  10.2 us
    dot_general x1, matrix products, local(): jnp.dot(padded_sequence[DILATION_STEP:DILATION_STEP + sequence_rows], fil...  9.74 us
    dot_general x1, matrix products, local(): jnp.dot(padded_sequence[0:sequence_rows], filter_weight[0], preferred_ele...  7.98 us
    all_to_all x1, starting transfers between devices, local(): lax.all_to_all(col_buffer, 'col', split_axis=0, concat_axis=0, tiled=True)  6.82 us
    ppermute x1, starting transfers between devices, with_halo(): lax.ppermute(tail, axis, [(i, (i + 1) % count) for i in range(ends)])  5.56 us
    all_to_all x1, waiting for transfers between devices, local(): lax.all_to_all(row_buffer, 'col', split_axis=0, concat_axis=0, tiled=True)  5.46 us
    scatter x1, other arithmetic, local(): jnp.zeros((slot_total_count, D), jnp.bfloat16).at[slot_index]  5.37 us
  transfers between devices with their start and end apart: 5, of which 1 were waited for; matrix products, arithmetic and copies ran while one was open for 18% of the time, Pallas kernels for 0%

commit v1 on v0

v1 whole, which is shorter than its diff:
```python
import functools

import jax
import jax.numpy as jnp
from jax import lax
from jax.experimental import pallas as pl
from jax.experimental.pallas import tpu as pltpu
from jax.sharding import PartitionSpec as P

DILATION_STEP = 32
POOL = 128
CAP = 64
LANES = 128
CHUNK = 256
PRE = 3
MESH = pl.DeviceIdType.MESH
F32 = jnp.float32
BF16 = jnp.bfloat16


def dot(a, b):
    return jnp.dot(a, b, preferred_element_type=F32)


def trunk(
    n_row,
    n_col,
    x_hbm,
    w_hbm,
    proj_ref,
    donor_ref,
    pos_ref,
    bin_ref,
    rows_out,
    cols_out,
    emb_out,
    coord_out,
    xbuf,
    wbuf,
    early,
    emb_acc,
    pooled,
    select,
    row_send,
    col_send,
    emb_send,
    coord_send,
    x_sem,
    w_sem,
    halo_send_sem,
    halo_recv_sem,
    coord_send_sem,
    coord_recv_sem,
    emb_send_sem,
    emb_recv_sem,
    row_send_sem,
    row_recv_sem,
    col_send_sem,
    col_recv_sem,
):
    rows, width = x_hbm.shape
    halo = DILATION_STEP
    chunks = width // CHUNK
    pre = min(PRE, chunks)
    bins = rows // POOL
    tile_cols = bins * n_row
    slots = n_col * CAP
    count = n_row * n_col
    my_row = lax.axis_index("row")
    my_col = lax.axis_index("col")
    me = my_row * n_col + my_col

    def place(flat):
        return (flat // n_col, lax.rem(flat, n_col))

    def w_copy(tap, n):
        return pltpu.make_async_copy(
            w_hbm.at[tap, :, pl.ds(pl.multiple_of(n * CHUNK, CHUNK), CHUNK)], wbuf.at[n, tap], w_sem.at[n, tap]
        )

    x_copy = pltpu.make_async_copy(x_hbm, xbuf.at[pl.ds(halo, rows)], x_sem)
    w_copy(1, 0).start()
    x_copy.start()
    for n in range(1, pre):
        w_copy(1, n).start()
    for n in range(chunks):
        w_copy(0, n).start()
        w_copy(2, n).start()
        if n + pre < chunks:
            w_copy(1, n + pre).start()

    has_left = me > 0
    has_right = me < count - 1
    col_home = me // n_row
    self_col = col_home == my_col
    barrier = pltpu.get_barrier_semaphore()

    @pl.when(has_left)
    def _():
        pl.semaphore_signal(barrier, inc=1, device_id=place(me - 1), device_id_type=MESH)

    @pl.when(has_right)
    def _():
        pl.semaphore_signal(barrier, inc=1, device_id=place(me + 1), device_id_type=MESH)

    for d in range(1, n_col):
        pl.semaphore_signal(barrier, inc=1, device_id=(my_row, lax.rem(my_col + d, n_col)), device_id_type=MESH)
    for i in range(n_row):
        source = my_col * n_row + i

        @pl.when(source != me)
        def _():
            pl.semaphore_signal(barrier, inc=1, device_id=place(source), device_id_type=MESH)

    pos = pos_ref[...]
    acceptor = bin_ref[...]
    listed = pos.shape[1]
    group = jnp.zeros_like(acceptor)
    for k in range(1, n_col):
        group = group + jnp.where(acceptor >= k * tile_cols, 1, 0)
    pair_col = acceptor - group * tile_cols
    kinds = max(16, n_col)
    in_group = lax.broadcasted_iota(jnp.int32, (kinds, listed), 0) == group
    before = lax.broadcasted_iota(jnp.int32, (listed, listed), 0) < lax.broadcasted_iota(jnp.int32, (listed, listed), 1)
    in_group = jnp.where(in_group, 1.0, 0.0)
    earlier = dot(in_group.astype(BF16), jnp.where(before, 1.0, 0.0).astype(BF16))
    rank = jnp.sum(in_group * earlier, axis=0, keepdims=True)
    slot = group.astype(F32) * float(CAP) + rank
    slot_hot = lax.broadcasted_iota(jnp.int32, (slots, listed), 0).astype(F32) == slot
    slot_hot = jnp.where(slot_hot, 1.0, 0.0).astype(BF16)

    def spread(hot):
        return lax.dot_general(
            slot_hot, jnp.where(hot, 1.0, 0.0).astype(BF16), (((1,), (1,)), ((), ())), preferred_element_type=F32
        ).astype(BF16)

    col_lanes = coord_send.shape[2] - LANES
    col_hot = lax.broadcasted_iota(jnp.int32, (col_lanes, listed), 0) == pair_col
    coord_send[:, :, :col_lanes] = spread(col_hot).reshape(n_col, CAP, col_lanes)
    base = lax.broadcasted_iota(jnp.int32, (LANES, listed), 0) * POOL
    row_hot = (pos >= base) & (pos < base + POOL)
    coord_send[:, :, col_lanes:] = spread(row_hot).reshape(n_col, CAP, LANES)
    select[...] = spread(lax.broadcasted_iota(jnp.int32, (rows, listed), 0) == pos)

    neighbours = jnp.where(has_left, 1, 0) + jnp.where(has_right, 1, 0)
    pl.semaphore_wait(barrier, neighbours + n_col - 1 + n_row - jnp.where(self_col, 1, 0))

    def up_copy():
        return pltpu.make_async_remote_copy(
            src_ref=x_hbm.at[pl.ds(0, halo)],
            dst_ref=xbuf.at[pl.ds(rows + halo, halo)],
            send_sem=halo_send_sem.at[0],
            recv_sem=halo_recv_sem.at[0],
            device_id=place(me - 1),
            device_id_type=MESH,
        )

    def down_copy():
        return pltpu.make_async_remote_copy(
            src_ref=x_hbm.at[pl.ds(rows - halo, halo)],
            dst_ref=xbuf.at[pl.ds(0, halo)],
            send_sem=halo_send_sem.at[1],
            recv_sem=halo_recv_sem.at[1],
            device_id=place(me + 1),
            device_id_type=MESH,
        )

    def row_group_copies(src, dst, send_sem, recv_sem, whole):
        copies = []
        for d in range(1, n_col):
            there = lax.rem(my_col + d, n_col)
            copies.append(
                pltpu.make_async_remote_copy(
                    src_ref=src if whole else src.at[there],
                    dst_ref=dst.at[my_col],
                    send_sem=send_sem.at[d - 1],
                    recv_sem=recv_sem.at[d - 1],
                    device_id=(my_row, there),
                    device_id_type=MESH,
                )
            )
        return copies

    def row_group_arrivals(src, dst, send_sem, recv_sem):
        for d in range(1, n_col):
            source = lax.rem(my_col + n_col - d, n_col)
            pltpu.make_async_remote_copy(
                src_ref=src,
                dst_ref=dst.at[source],
                send_sem=send_sem.at[d - 1],
                recv_sem=recv_sem.at[d - 1],
                device_id=(my_row, source),
                device_id_type=MESH,
            ).wait_recv()

    @pl.when(has_left)
    def _():
        up_copy().start()

    @pl.when(has_right)
    def _():
        down_copy().start()

    coord_copies = row_group_copies(coord_send, coord_out, coord_send_sem, coord_recv_sem, False)
    for copy in coord_copies:
        copy.start()
    coord_out[my_col] = coord_send[my_col]

    @pl.when(jnp.logical_not(has_left))
    def _():
        xbuf[0:halo] = jnp.zeros((halo, width), BF16)

    @pl.when(jnp.logical_not(has_right))
    def _():
        xbuf[rows + halo : rows + 2 * halo] = jnp.zeros((halo, width), BF16)

    x_copy.wait()

    def centre(n, carry):
        w_copy(1, n).wait()
        early[n] = dot(xbuf[halo : halo + rows], wbuf[n, 1])
        return carry

    lax.fori_loop(0, pre, centre, 0)

    @pl.when(has_left)
    def _():
        down = down_copy()
        down.wait_recv()

    @pl.when(has_right)
    def _():
        up = up_copy()
        up.wait_recv()

    emb_acc[...] = jnp.zeros_like(emb_acc)

    def finish(n, base, with_centre):
        w_copy(0, n).wait()
        w_copy(2, n).wait()
        if with_centre:
            w_copy(1, n).wait()
        cols = pl.ds(pl.multiple_of(n * CHUNK, CHUNK), CHUNK)
        total = dot(xbuf[0:rows], wbuf[n, 0]) + dot(xbuf[2 * halo : 2 * halo + rows], wbuf[n, 2])
        if with_centre:
            total = total + dot(xbuf[halo : halo + rows], wbuf[n, 1])
        else:
            total = total + base
        half = 0.5 * total
        hidden = (xbuf[halo : halo + rows, cols].astype(F32) + (half + half * jnp.tanh(half))).astype(BF16)
        pooled[:, cols] = jnp.sum(hidden.astype(F32).reshape(bins, POOL, CHUNK), axis=1) * (1.0 / POOL)
        emb_acc[...] += dot(hidden, donor_ref[cols, :])

    def first(n, carry):
        finish(n, early[n], False)
        return carry

    def rest(n, carry):
        finish(n, None, True)
        return carry

    lax.fori_loop(0, pre, first, 0)
    lax.fori_loop(pre, chunks, rest, 0)

    means = pooled[...]
    scale = lax.rsqrt(jnp.mean(means * means, axis=-1, keepdims=True) + 1e-06)
    projected = dot((means * scale).astype(BF16), proj_ref[...]).astype(BF16).astype(F32)
    row_send[...] = projected[:, :LANES]
    col_send[...] = projected[:, LANES:]

    my_slot = me - col_home * n_row

    def col_copy(r):
        return pltpu.make_async_remote_copy(
            src_ref=col_send,
            dst_ref=cols_out.at[my_slot],
            send_sem=col_send_sem.at[r],
            recv_sem=col_recv_sem.at[my_slot],
            device_id=(r, col_home),
            device_id_type=MESH,
        )

    def is_other(r):
        return jnp.logical_or(jnp.logical_not(self_col), my_row != r)

    for r in range(n_row):

        @pl.when(is_other(r))
        def _():
            col_copy(r).start()

    row_copies = row_group_copies(row_send, rows_out, row_send_sem, row_recv_sem, True)
    for copy in row_copies:
        copy.start()

    emb_send[...] = dot(select[...], emb_acc[...].astype(BF16)).astype(BF16).reshape(n_col, CAP, LANES)
    emb_copies = row_group_copies(emb_send, emb_out, emb_send_sem, emb_recv_sem, False)
    for copy in emb_copies:
        copy.start()
    emb_out[my_col] = emb_send[my_col]
    rows_out[my_col] = row_send[...]

    @pl.when(self_col)
    def _():
        cols_out[my_slot] = col_send[...]

    row_group_arrivals(coord_send.at[0], coord_out, coord_send_sem, coord_recv_sem)
    row_group_arrivals(row_send, rows_out, row_send_sem, row_recv_sem)
    row_group_arrivals(emb_send.at[0], emb_out, emb_send_sem, emb_recv_sem)
    for i in range(n_row):
        source = my_col * n_row + i

        @pl.when(source != me)
        def _():
            pltpu.make_async_remote_copy(
                src_ref=col_send,
                dst_ref=cols_out.at[i],
                send_sem=col_send_sem.at[i],
                recv_sem=col_recv_sem.at[i],
                device_id=place(source),
                device_id_type=MESH,
            ).wait_recv()

    for copy in coord_copies + row_copies + emb_copies:
        copy.wait_send()
    for r in range(n_row):

        @pl.when(is_other(r))
        def _():
            col_copy(r).wait_send()

    @pl.when(has_left)
    def _():
        up_copy().wait_send()

    @pl.when(has_right)
    def _():
        down_copy().wait_send()


def tiles(rows_ref, cols_ref, emb_ref, coord_ref, out_ref, pair_ref, junction_ref):
    n_col, bins, lanes = rows_ref.shape
    n_row = cols_ref.shape[0]
    tile_rows, tile_cols = n_col * bins, n_row * bins
    row_side = rows_ref[...].reshape(tile_rows, lanes)
    col_side = cols_ref[...].reshape(tile_cols, lanes)
    weight = out_ref[...]
    cap = emb_ref.shape[1]
    col_lanes = coord_ref.shape[2] - lanes
    side = min(8, tile_rows)
    for i in range(tile_rows // side):
        hidden = jnp.maximum(row_side[i * side : (i + 1) * side, None, :] + col_side[None, :, :], 0.0).astype(BF16)
        pair_ref[i * side : (i + 1) * side] = (
            dot(hidden.reshape(side * tile_cols, lanes), weight).astype(BF16).reshape(side, tile_cols, lanes)
        )
    coord = coord_ref[...]
    by_col = dot(coord[:, :, :tile_cols].reshape(n_col * cap, tile_cols), col_side.astype(BF16))
    by_row = [dot(coord[k, :, col_lanes : col_lanes + bins], rows_ref[k].astype(BF16)) for k in range(n_col)]
    hidden = jnp.maximum(jnp.concatenate(by_row, axis=0) + by_col, 0.0).astype(BF16)
    looked = dot(hidden, weight).astype(BF16)
    emb = emb_ref[...].reshape(n_col * cap, lanes)
    junction_ref[...] = jnp.maximum(emb.astype(F32) + looked.astype(F32), 0.0).astype(BF16)


def local(n_row, n_col, sequence, filter_weight, pair_proj, pair_out, donor_w, donor_pos, acceptor_bin):
    rows, width = sequence.shape
    lanes = pair_out.shape[0]
    bins = rows // POOL
    listed = donor_pos.shape[0]
    chunks = width // CHUNK
    tile_rows, tile_cols = bins * n_col, bins * n_row
    col_lanes = -(-tile_cols // LANES) * LANES
    slots = n_col * CAP
    vmem = pl.BlockSpec(memory_space=pltpu.VMEM)
    hbm = pl.BlockSpec(memory_space=pl.ANY)
    dma = pltpu.SemaphoreType.DMA
    arrived = pl.pallas_call(
        functools.partial(trunk, n_row, n_col),
        out_shape=(
            jax.ShapeDtypeStruct((n_col, bins, lanes), F32),
            jax.ShapeDtypeStruct((n_row, bins, lanes), F32),
            jax.ShapeDtypeStruct((n_col, CAP, lanes), BF16),
            jax.ShapeDtypeStruct((n_col, CAP, col_lanes + LANES), BF16),
        ),
        in_specs=[hbm, hbm, vmem, vmem, vmem, vmem],
        out_specs=(vmem, vmem, vmem, vmem),
        scratch_shapes=[
            pltpu.VMEM((rows + 2 * DILATION_STEP, width), BF16),
            pltpu.VMEM((chunks, 3, width, CHUNK), BF16),
            pltpu.VMEM((min(PRE, chunks), rows, CHUNK), F32),
            pltpu.VMEM((rows, lanes), F32),
            pltpu.VMEM((bins, width), F32),
            pltpu.VMEM((slots, rows), BF16),
            pltpu.VMEM((bins, lanes), F32),
            pltpu.VMEM((bins, lanes), F32),
            pltpu.VMEM((n_col, CAP, lanes), BF16),
            pltpu.VMEM((n_col, CAP, col_lanes + LANES), BF16),
            dma,
            dma((chunks, 3)),
            dma((2,)),
            dma((2,)),
            dma((n_col - 1,)),
            dma((n_col - 1,)),
            dma((n_col - 1,)),
            dma((n_col - 1,)),
            dma((n_col - 1,)),
            dma((n_col - 1,)),
            dma((n_row,)),
            dma((n_row,)),
        ],
        compiler_params=pltpu.CompilerParams(
            collective_id=0, has_side_effects=True, vmem_limit_bytes=56 * 1024 * 1024
        ),
        name="trunk",
    )(
        sequence,
        filter_weight,
        pair_proj,
        donor_w,
        donor_pos.reshape(1, listed),
        acceptor_bin.reshape(1, listed),
    )
    return pl.pallas_call(
        tiles,
        out_shape=(
            jax.ShapeDtypeStruct((tile_rows, tile_cols, lanes), BF16),
            jax.ShapeDtypeStruct((slots, lanes), BF16),
        ),
        in_specs=[vmem] * 5,
        out_specs=(vmem, vmem),
        name="tiles",
    )(*arrived, pair_out)


def solution(mesh):
    placed = (P(("row", "col"), None), P(), P(), P(), P(), P(("row", "col")), P(("row", "col")))
    return jax.shard_map(
        functools.partial(local, mesh.shape["row"], mesh.shape["col"]),
        mesh=mesh,
        in_specs=placed,
        out_specs=(P("row", "col", None), P(("row", "col"), None)),
        check_vma=False,
    )
```

time: 162 us -> 38.3 us (0.24)
  blocking collectives: 84.1 us -> 0 us
  Pallas kernels: 0 us -> 37.5 us
  matrix products: 33 us -> 0 us
  starting transfers between devices: 22.3 us -> 0 us
  other arithmetic: 9.59 us -> 0 us
  local copies, waits for them, and re-layouts: 6.52 us -> 0 us
  waiting for transfers between devices: 5.47 us -> 0 us
    all_gather x1 -> x0, blocking collectives: 84.1 us -> none  [local(): gathered = lax.all_gather(normed, ('row', 'col'), axis=0, tiled=True)]
    pallas_call x0 -> x2, Pallas kernels: none -> 37.5 us  [the longest x1 35.4 us: local(): pl.pallas_call(functools.partial(trunk, n_row, n_col), out_shape=(jax.Sha...]
    dot_general x7 -> x0, matrix products: 33 us -> none  [the longest x1 10.2 us: local(): jnp.dot(padded_sequence[2 * DILATION_STEP:2 * DILATION_STEP + sequence_ro...]
    all_to_all x3 -> x0, starting transfers between devices: 15.4 us -> none  [the longest x1 6.82 us: local(): lax.all_to_all(col_buffer, 'col', split_axis=0, concat_axis=0, tiled=True)]
    ppermute x2 -> x0, starting transfers between devices: 6.85 us -> none  [the longest x1 5.56 us: with_halo(): lax.ppermute(tail, axis, [(i, (i + 1) % count) for i in range(ends)])]
    all_to_all x3 -> x0, waiting for transfers between devices: 5.46 us -> none  [the longest x1 5.46 us: local(): lax.all_to_all(row_buffer, 'col', split_axis=0, concat_axis=0, tiled=True)]
    scatter x1 -> x0, other arithmetic: 5.37 us -> none  [local(): jnp.zeros((slot_total_count, D), jnp.bfloat16).at[slot_index]]
    scatter x2 -> x0, local copies, waits for them, and re-layouts: 2.79 us -> none  [the longest x1 1.4 us: local(): jnp.full((slot_total_count,), -1, jnp.int32).at[slot_index].set(pair_col)]
  transfers between devices with their start and end apart: 5 -> 0, of which waited for: 1 -> 0; matrix products, arithmetic and copies ran while one was open for 18% -> 0% of each run, Pallas kernels for 0% -> 0%
where the time goes in v1:
time: 38.3 us; the launch traced here: 38.1 us
  Pallas kernels  37.5 us (98%)
  between operations  0.64 us (2%)
    pallas_call x1, Pallas kernels, local(): pl.pallas_call(functools.partial(trunk, n_row, n_col), out_shape=(jax.Sha...  35.4 us
    pallas_call x1, Pallas kernels, local(): pl.pallas_call(tiles, out_shape=(jax.ShapeDtypeStruct((tile_rows, tile_co...  2.08 us

profile of v1, /device:TPU:0, one launch (start us, length us, event | category | flops | bytes accessed | tf_op | source)
XLA Modules:
  0.0 38.1 jit_solution(5936066535483826664)
XLA Ops:
  0.6 35.4 %trunk.1 = (f32[4,8,128]{2,1,0:T(8,128)}, f32[8,8,128]{2,1,0:T(8,128)}, bf16[4,64,128]{2,1,0:T(8,128)(2,1)}, bf16[4,64,256]{2,1,0:T(8,128)(2,1)}) custom-call(bf16[1024,1536]{1,0:T(8,128)(2,1)} %x_hbm.1, bf16[3,1536,1536]{2,1,0:T(8,128)(2,1)} %w_hbm.1, bf16[1536,256]{1,0:T(8,128)(2,1)} %proj_ref.1, bf16[1536,128]{1,0:T(8,128)(2,1)} %donor_ref.1, ...), custom_call_target="tpu_custom_call" | custom-call | tf_op jit(solution)/shard_map/trunk/pallas_call | solution.py:377
  36.0 2.1 %tiles.1 = (bf16[32,64,128]{2,1,0:T(8,128)(2,1)}, bf16[256,128]{1,0:T(8,128)(2,1)}) custom-call(f32[4,8,128]{2,1,0:T(8,128)} %get-tuple-element.6.rows_ref, f32[8,8,128]{2,1,0:T(8,128)} %get-tuple-element.7.cols_ref, bf16[4,64,128]{2,1,0:T(8,128)(2,1)} %get-tuple-element.8.emb_ref, bf16[4,64,256]{2,1,0:T(8,128)(2,1)} %get-tuple-element.9.coord_ref, ...), custom_call_target="tpu_custom_call" | custom-call | tf_op jit(solution)/shard_map/tiles/pallas_call | solution.py:423

commit v2 on v1

--- a/solution.py
+++ b/solution.py
@@ -11,8 +11,9 @@
 POOL = 128
 CAP = 64
 LANES = 128
-CHUNK = 256
-PRE = 3
+CHUNK = 512
+BLOCK = 256
+PRE = 1
 MESH = pl.DeviceIdType.MESH
 F32 = jnp.float32
 BF16 = jnp.bfloat16
@@ -27,8 +28,8 @@
     n_col,
     x_hbm,
     w_hbm,
-    proj_ref,
-    donor_ref,
+    proj_hbm,
+    donor_hbm,
     pos_ref,
     bin_ref,
     rows_out,
@@ -37,15 +38,17 @@
     coord_out,
     xbuf,
     wbuf,
-    early,
-    emb_acc,
+    hidden,
     pooled,
     select,
+    proj_ref,
+    donor_ref,
     row_send,
     col_send,
     emb_send,
     coord_send,
     x_sem,
+    end_sem,
     w_sem,
     halo_send_sem,
     halo_recv_sem,
@@ -75,19 +78,18 @@
 
     def w_copy(tap, n):
         return pltpu.make_async_copy(
-            w_hbm.at[tap, :, pl.ds(pl.multiple_of(n * CHUNK, CHUNK), CHUNK)], wbuf.at[n, tap], w_sem.at[n, tap]
+            w_hbm.at[tap, :, pl.ds(pl.multiple_of(n * CHUNK, CHUNK), CHUNK)], wbuf.at[n, pl.ds(tap * width, width)], w_sem.at[n, tap]
         )
 
     x_copy = pltpu.make_async_copy(x_hbm, xbuf.at[pl.ds(halo, rows)], x_sem)
-    w_copy(1, 0).start()
     x_copy.start()
-    for n in range(1, pre):
-        w_copy(1, n).start()
     for n in range(chunks):
-        w_copy(0, n).start()
-        w_copy(2, n).start()
-        if n + pre < chunks:
-            w_copy(1, n + pre).start()
+        for tap in range(3):
+            w_copy(tap, n).start()
+    proj_copy = pltpu.make_async_copy(proj_hbm, proj_ref, end_sem.at[0])
+    donor_copy = pltpu.make_async_copy(donor_hbm, donor_ref, end_sem.at[1])
+    proj_copy.start()
+    donor_copy.start()
 
     has_left = me > 0
     has_right = me < count - 1
@@ -216,52 +218,55 @@
 
     x_copy.wait()
 
-    def centre(n, carry):
-        w_copy(1, n).wait()
-        early[n] = dot(xbuf[halo : halo + rows], wbuf[n, 1])
+    def block(n, start):
+        cols = pl.ds(pl.multiple_of(n * CHUNK, CHUNK), CHUNK)
+        taps = [xbuf[start + tap * halo : start + tap * halo + BLOCK] for tap in range(3)]
+        total = dot(jnp.concatenate(taps, axis=1), wbuf[n])
+        half = 0.5 * total
+        centre = xbuf[start + halo : start + halo + BLOCK, cols].astype(F32)
+        out = (centre + (half + half * jnp.tanh(half))).astype(BF16)
+        hidden[start : start + BLOCK, cols] = out
+        first = start // POOL
+        pooled[first : first + BLOCK // POOL, cols] = jnp.sum(
+            out.astype(F32).reshape(BLOCK // POOL, POOL, CHUNK), axis=1
+        ) * (1.0 / POOL)
+
+    starts = list(range(0, rows, BLOCK))
+
+    def inner(n, carry):
+        for tap in range(3):
+            w_copy(tap, n).wait()
+        for start in starts[1:-1]:
+            block(n, start)
         return carry
 
-    lax.fori_loop(0, pre, centre, 0)
+    lax.fori_loop(0, pre, inner, 0)
 
     @pl.when(has_left)
     def _():
-        down = down_copy()
-        down.wait_recv()
+        down_copy().wait_recv()
 
     @pl.when(has_right)
     def _():
-        up = up_copy()
-        up.wait_recv()
-
-    emb_acc[...] = jnp.zeros_like(emb_acc)
-
-    def finish(n, base, with_centre):
-        w_copy(0, n).wait()
-        w_copy(2, n).wait()
-        if with_centre:
-            w_copy(1, n).wait()
-        cols = pl.ds(pl.multiple_of(n * CHUNK, CHUNK), CHUNK)
-        total = dot(xbuf[0:rows], wbuf[n, 0]) + dot(xbuf[2 * halo : 2 * halo + rows], wbuf[n, 2])
-        if with_centre:
-            total = total + dot(xbuf[halo : halo + rows], wbuf[n, 1])
-        else:
-            total = total + base
-        half = 0.5 * total
-        hidden = (xbuf[halo : halo + rows, cols].astype(F32) + (half + half * jnp.tanh(half))).astype(BF16)
-        pooled[:, cols] = jnp.sum(hidden.astype(F32).reshape(bins, POOL, CHUNK), axis=1) * (1.0 / POOL)
-        emb_acc[...] += dot(hidden, donor_ref[cols, :])
-
-    def first(n, carry):
-        finish(n, early[n], False)
+        up_copy().wait_recv()
+
+    def outer(n, carry):
+        for start in (starts[0], starts[-1]):
+            block(n, start)
         return carry
 
     def rest(n, carry):
-        finish(n, None, True)
+        for tap in range(3):
+            w_copy(tap, n).wait()
+        for start in starts:
+            block(n, start)
         return carry
 
-    lax.fori_loop(0, pre, first, 0)
+    lax.fori_loop(0, pre, outer, 0)
     lax.fori_loop(pre, chunks, rest, 0)
 
+    proj_copy.wait()
+    donor_copy.wait()
     means = pooled[...]
     scale = lax.rsqrt(jnp.mean(means * means, axis=-1, keepdims=True) + 1e-06)
     projected = dot((means * scale).astype(BF16), proj_ref[...]).astype(BF16).astype(F32)
@@ -293,7 +298,7 @@
     for copy in row_copies:
         copy.start()
 
-    emb_send[...] = dot(select[...], emb_acc[...].astype(BF16)).astype(BF16).reshape(n_col, CAP, LANES)
+    emb_send[...] = dot(select[...], dot(hidden[...], donor_ref[...]).astype(BF16)).astype(BF16).reshape(n_col, CAP, LANES)
     emb_copies = row_group_copies(emb_send, emb_out, emb_send_sem, emb_recv_sem, False)
     for copy in emb_copies:
         copy.start()
@@ -382,20 +387,22 @@
             jax.ShapeDtypeStruct((n_col, CAP, lanes), BF16),
             jax.ShapeDtypeStruct((n_col, CAP, col_lanes + LANES), BF16),
         ),
-        in_specs=[hbm, hbm, vmem, vmem, vmem, vmem],
+        in_specs=[hbm, hbm, hbm, hbm, vmem, vmem],
         out_specs=(vmem, vmem, vmem, vmem),
         scratch_shapes=[
             pltpu.VMEM((rows + 2 * DILATION_STEP, width), BF16),
-            pltpu.VMEM((chunks, 3, width, CHUNK), BF16),
-            pltpu.VMEM((min(PRE, chunks), rows, CHUNK), F32),
-            pltpu.VMEM((rows, lanes), F32),
+            pltpu.VMEM((chunks, 3 * width, CHUNK), BF16),
+            pltpu.VMEM((rows, width), BF16),
             pltpu.VMEM((bins, width), F32),
             pltpu.VMEM((slots, rows), BF16),
+            pltpu.VMEM(pair_proj.shape, BF16),
+            pltpu.VMEM(donor_w.shape, BF16),
             pltpu.VMEM((bins, lanes), F32),
             pltpu.VMEM((bins, lanes), F32),
             pltpu.VMEM((n_col, CAP, lanes), BF16),
             pltpu.VMEM((n_col, CAP, col_lanes + LANES), BF16),
             dma,
+            dma((2,)),
             dma((chunks, 3)),
             dma((2,)),
             dma((2,)),

time: 38.3 us -> 35.4 us (0.924)
  Pallas kernels: 37.5 us -> 34.6 us
    pallas_call x1, Pallas kernels: 35.4 us -> 32.5 us  [local(): pl.pallas_call(functools.partial(trunk, n_row, n_col), out_shape=(jax.Sha...]
where the time goes in v2:
time: 35.4 us; the launch traced here: 35.2 us
  Pallas kernels  34.6 us (98%)
  between operations  0.64 us (2%)
    pallas_call x1, Pallas kernels, local(): pl.pallas_call(functools.partial(trunk, n_row, n_col), out_shape=(jax.Sha...  32.5 us
    pallas_call x1, Pallas kernels, local(): pl.pallas_call(tiles, out_shape=(jax.ShapeDtypeStruct((tile_rows, tile_co...  2.08 us

profile of v2, /device:TPU:0, one launch (start us, length us, event | category | flops | bytes accessed | tf_op | source)
XLA Modules:
  0.0 35.2 jit_solution(2608971224054803607)
XLA Ops:
  0.6 32.5 %trunk.1 = (f32[4,8,128]{2,1,0:T(8,128)}, f32[8,8,128]{2,1,0:T(8,128)}, bf16[4,64,128]{2,1,0:T(8,128)(2,1)}, bf16[4,64,256]{2,1,0:T(8,128)(2,1)}) custom-call(bf16[1024,1536]{1,0:T(8,128)(2,1)} %x_hbm.1, bf16[3,1536,1536]{2,1,0:T(8,128)(2,1)} %w_hbm.1, bf16[1536,256]{1,0:T(8,128)(2,1)} %proj_hbm.1, bf16[1536,128]{1,0:T(8,128)(2,1)} %donor_hbm.1, ...), custom_call_target="tpu_custom_call" | custom-call | tf_op jit(solution)/shard_map/trunk/pallas_call | solution.py:382
  33.1 2.1 %tiles.1 = (bf16[32,64,128]{2,1,0:T(8,128)(2,1)}, bf16[256,128]{1,0:T(8,128)(2,1)}) custom-call(f32[4,8,128]{2,1,0:T(8,128)} %get-tuple-element.6.rows_ref, f32[8,8,128]{2,1,0:T(8,128)} %get-tuple-element.7.cols_ref, bf16[4,64,128]{2,1,0:T(8,128)(2,1)} %get-tuple-element.8.emb_ref, bf16[4,64,256]{2,1,0:T(8,128)(2,1)} %get-tuple-element.9.coord_ref, ...), custom_call_target="tpu_custom_call" | custom-call | tf_op jit(solution)/shard_map/tiles/pallas_call | solution.py:430

commit v3 on v2

--- a/solution.py
+++ b/solution.py
@@ -13,7 +13,7 @@
 LANES = 128
 CHUNK = 512
 BLOCK = 256
-PRE = 1
+PRE = 2
 MESH = pl.DeviceIdType.MESH
 F32 = jnp.float32
 BF16 = jnp.bfloat16
@@ -76,6 +76,29 @@
     def place(flat):
         return (flat // n_col, lax.rem(flat, n_col))
 
+    has_left = me > 0
+    has_right = me < count - 1
+    col_home = me // n_row
+    self_col = col_home == my_col
+    barrier = pltpu.get_barrier_semaphore()
+
+    @pl.when(has_left)
+    def _():
+        pl.semaphore_signal(barrier, inc=1, device_id=place(me - 1), device_id_type=MESH)
+
+    @pl.when(has_right)
+    def _():
+        pl.semaphore_signal(barrier, inc=1, device_id=place(me + 1), device_id_type=MESH)
+
+    for d in range(1, n_col):
+        pl.semaphore_signal(barrier, inc=1, device_id=(my_row, lax.rem(my_col + d, n_col)), device_id_type=MESH)
+    for i in range(n_row):
+        source = my_col * n_row + i
+
+        @pl.when(source != me)
+        def _():
+            pl.semaphore_signal(barrier, inc=1, device_id=place(source), device_id_type=MESH)
+
     def w_copy(tap, n):
         return pltpu.make_async_copy(
             w_hbm.at[tap, :, pl.ds(pl.multiple_of(n * CHUNK, CHUNK), CHUNK)], wbuf.at[n, pl.ds(tap * width, width)], w_sem.at[n, tap]
@@ -90,29 +113,6 @@
     donor_copy = pltpu.make_async_copy(donor_hbm, donor_ref, end_sem.at[1])
     proj_copy.start()
     donor_copy.start()
-
-    has_left = me > 0
-    has_right = me < count - 1
-    col_home = me // n_row
-    self_col = col_home == my_col
-    barrier = pltpu.get_barrier_semaphore()
-
-    @pl.when(has_left)
-    def _():
-        pl.semaphore_signal(barrier, inc=1, device_id=place(me - 1), device_id_type=MESH)
-
-    @pl.when(has_right)
-    def _():
-        pl.semaphore_signal(barrier, inc=1, device_id=place(me + 1), device_id_type=MESH)
-
-    for d in range(1, n_col):
-        pl.semaphore_signal(barrier, inc=1, device_id=(my_row, lax.rem(my_col + d, n_col)), device_id_type=MESH)
-    for i in range(n_row):
-        source = my_col * n_row + i
-
-        @pl.when(source != me)
-        def _():
-            pl.semaphore_signal(barrier, inc=1, device_id=place(source), device_id_type=MESH)
 
     pos = pos_ref[...]
     acceptor = bin_ref[...]

time: 35.4 us -> 35.6 us (level)
  no operation moved by 1% of the time
where the time goes in v3:
time: 35.6 us; the launch traced here: 35.4 us
  Pallas kernels  34.7 us (97%)
  between operations  0.64 us (2%)
    pallas_call x1, Pallas kernels, local(): pl.pallas_call(functools.partial(trunk, n_row, n_col), out_shape=(jax.Sha...  32.7 us
    pallas_call x1, Pallas kernels, local(): pl.pallas_call(tiles, out_shape=(jax.ShapeDtypeStruct((tile_rows, tile_co...  2.08 us

profile of v3, /device:TPU:0, one launch (start us, length us, event | category | flops | bytes accessed | tf_op | source)
XLA Modules:
  0.0 35.4 jit_solution(5311804871913931704)
XLA Ops:
  0.6 32.7 %trunk.1 = (f32[4,8,128]{2,1,0:T(8,128)}, f32[8,8,128]{2,1,0:T(8,128)}, bf16[4,64,128]{2,1,0:T(8,128)(2,1)}, bf16[4,64,256]{2,1,0:T(8,128)(2,1)}) custom-call(bf16[1024,1536]{1,0:T(8,128)(2,1)} %x_hbm.1, bf16[3,1536,1536]{2,1,0:T(8,128)(2,1)} %w_hbm.1, bf16[1536,256]{1,0:T(8,128)(2,1)} %proj_hbm.1, bf16[1536,128]{1,0:T(8,128)(2,1)} %donor_hbm.1, ...), custom_call_target="tpu_custom_call" | custom-call | tf_op jit(solution)/shard_map/trunk/pallas_call | solution.py:382
  33.3 2.1 %tiles.1 = (bf16[32,64,128]{2,1,0:T(8,128)(2,1)}, bf16[256,128]{1,0:T(8,128)(2,1)}) custom-call(f32[4,8,128]{2,1,0:T(8,128)} %get-tuple-element.6.rows_ref, f32[8,8,128]{2,1,0:T(8,128)} %get-tuple-element.7.cols_ref, bf16[4,64,128]{2,1,0:T(8,128)(2,1)} %get-tuple-element.8.emb_ref, bf16[4,64,256]{2,1,0:T(8,128)(2,1)} %get-tuple-element.9.coord_ref, ...), custom_call_target="tpu_custom_call" | custom-call | tf_op jit(solution)/shard_map/tiles/pallas_call | solution.py:430
